TPU v7x, 32 devices: a whole 2x2x4 slice. The times are simulated.
32 devices in a mesh: ctx: 4 (over y, x), dp: 8 (over z, core).
Axes of the slice: x: 2, y: 2, z: 4, core: 2. Of those that a mesh axis runs over, the one named last changes fastest.
Arguments:
- queries: bfloat16 [8, 512, 1024], P('dp', 'ctx'), may hold values from -6 to 6
- keys_in: bfloat16 [8, 512, 256], P('dp', 'ctx'), may hold values from -6 to 6
- values_in: bfloat16 [8, 512, 256], P('dp', 'ctx'), may hold values from -6 to 6
- patch_order: int32 [8, 4, 128], P('dp', 'ctx'), may hold values from 0 to 127, each once within a row
- block_mask: int32 [8, 16, 8], P('dp', 'ctx'), may hold values 0 or 1
- out_weight: bfloat16 [1024, 1024], P('dp'), may hold values from -0.1875 to 0.1875
- cotangent: bfloat16 [8, 512, 1024], P('dp', 'ctx'), may hold values from -6 to 6
Outputs:
- mixed: bfloat16 [8, 512, 1024], P('dp', 'ctx')
- grad_queries: bfloat16 [8, 512, 1024], P('dp', 'ctx')
- grad_keys: bfloat16 [8, 512, 256], P('dp', 'ctx')
- grad_values: bfloat16 [8, 512, 256], P('dp', 'ctx')
- grad_weight: float32 [1024, 1024], P('dp', 'ctx')
Inputs may be any that keep to these rules, and one draw needn't show every extreme that they name: `patch_order`: each row of 128 entries is a permutation.
All inputs are finite; a program needn't handle non-finite values. No bound on the sum of `block_mask` on one device may be relied on, other than what follows from the above.
Results may differ from a plain program's by a relative error of at most 0.015.
Values may be sent and summed in bfloat16 or wider, within the bound.
No kernel may reach another device: no remote copies, remote signals or barrier semaphores. Data moves between devices by JAX's collectives and lax.ppermute only.
A program may use at most 64 MiB of HBM per device.

v0:
```python
import functools
import math

import jax
import jax.numpy as jnp
from jax import lax
from jax.experimental import pallas as pl
from jax.experimental.pallas import tpu as pltpu
from jax.sharding import PartitionSpec as P

QUERY_HEADS = 8
KEY_VALUE_HEADS = 2
HEAD_WIDTH = 128
BLK = 32
HALO_ROWS = 8


F32 = jnp.float32
BF16 = jnp.bfloat16
NN = (((1,), (0,)), ((), ()))
NT = (((1,), (1,)), ((), ()))
TN = (((0,), (0,)), ((), ()))


def dot(a, b, dims):
    return lax.dot_general(a, b, dims, preferred_element_type=F32)


def vmem():
    return pl.BlockSpec(memory_space=pltpu.VMEM)


def smem():
    return pl.BlockSpec(memory_space=pltpu.SMEM)


def hbm():
    return pl.BlockSpec(memory_space=pltpu.HBM)


def in_hbm(*arrays):
    return tuple(pltpu.with_memory_space_constraint(a, pltpu.HBM) for a in arrays)


def call(body, outs, specs, args, scratch=(), flops=1 << 20, room=16 << 20):
    moved = sum(a.size * a.dtype.itemsize for a in (*args, *outs))
    return pl.pallas_call(
        body,
        out_shape=outs,
        in_specs=specs,
        out_specs=[vmem() for _ in outs],
        scratch_shapes=list(scratch),
        cost_estimate=pl.CostEstimate(flops=flops, bytes_accessed=moved, transcendentals=0),
        compiler_params=pltpu.CompilerParams(vmem_limit_bytes=room),
    )(*args)


def shape(dims, dtype=BF16):
    return jax.ShapeDtypeStruct(dims, dtype)


def pack_body(k_ref, v_ref, order_ref, out_ref, order_scr, sem):
    tokens, width = k_ref.shape
    copies = [
        pltpu.make_async_copy(order_ref, order_scr, sem.at[0]),
        pltpu.make_async_copy(k_ref, out_ref.at[:tokens, :width], sem.at[1]),
        pltpu.make_async_copy(v_ref, out_ref.at[:tokens, width:], sem.at[2]),
    ]
    for c in copies:
        c.start()
    copies[0].wait()
    row = lax.broadcasted_iota(jnp.int32, (tokens, tokens), 0)
    holds = (row == order_scr[...]).astype(F32).astype(BF16)
    block = lax.broadcasted_iota(jnp.int32, (HALO_ROWS, tokens), 1) // BLK
    out_ref[tokens:, :] = jnp.zeros((HALO_ROWS, 2 * width), BF16)
    out_ref[tokens:, :tokens] = dot(block.astype(F32).astype(BF16), holds, NT).astype(BF16)
    copies[1].wait()
    copies[2].wait()


def fetch_body(a_ref, b_ref, a_out, b_out, sem):
    copies = [
        pltpu.make_async_copy(a_ref, a_out, sem.at[0]),
        pltpu.make_async_copy(b_ref, b_out, sem.at[1]),
    ]
    for c in copies:
        c.start()
    for c in copies:
        c.wait()


def seen(mask_ref, first, key_block, query_block):
    sub = lax.broadcasted_iota(jnp.int32, key_block.shape, 0)
    blocks = mask_ref.shape[1] // 2
    table = jnp.zeros(key_block.shape, F32)
    for b in range(mask_ref.shape[0]):
        for kb in range(blocks):
            here = (sub == b) & (key_block == kb)
            table = jnp.where(here, mask_ref[b, first + kb].astype(F32), table)
    one_hot = (sub == query_block).astype(F32)
    return dot(table.astype(BF16), one_hot.astype(BF16), TN)


def forward_body(scale, q_ref, prev_ref, own_ref, next_ref, mask_ref, prob_ref, attf_ref, att_ref):
    tokens = q_ref.shape[0]
    width = own_ref.shape[1] // 2
    group = QUERY_HEADS // KEY_VALUE_HEADS
    blocks = mask_ref.shape[1] // 2
    ids = [r[tokens:, :tokens].astype(F32).astype(jnp.int32) for r in (prev_ref, own_ref, next_ref)]
    see_prev = seen(mask_ref, 0, ids[0], ids[1]) > 0.5
    see_next = seen(mask_ref, blocks, ids[2], ids[1]) > 0.5
    for g in range(KEY_VALUE_HEADS):
        cols = slice(g * HEAD_WIDTH, (g + 1) * HEAD_WIDTH)
        vcols = slice(width + g * HEAD_WIDTH, width + (g + 1) * HEAD_WIDTH)
        keys = jnp.concatenate([r[:tokens, cols] for r in (prev_ref, own_ref, next_ref)], 0)
        values = jnp.concatenate([r[:tokens, vcols] for r in (prev_ref, own_ref, next_ref)], 0)
        values_t = values.T
        for j in range(group):
            h = g * group + j
            at = slice(h * HEAD_WIDTH, (h + 1) * HEAD_WIDTH)
            scores = dot(keys, q_ref[:, at], NT) * scale
            low = jnp.where(see_prev, scores[:tokens], -1e30)
            mid = scores[tokens : 2 * tokens]
            high = jnp.where(see_next, scores[2 * tokens :], -1e30)
            top = jnp.maximum(jnp.maximum(low, mid), high).max(axis=0, keepdims=True)
            low, mid, high = jnp.exp(low - top), jnp.exp(mid - top), jnp.exp(high - top)
            inverse = 1.0 / (low + mid + high).sum(axis=0, keepdims=True)
            prob = jnp.concatenate([(low * inverse), (mid * inverse), (high * inverse)], 0).astype(BF16)
            prob_ref[:, at] = prob
            att = dot(values_t, prob, NN)
            attf_ref[at, :] = att
            att_ref[at, :] = att.astype(BF16)


def split_body(att_ref, keep_ref, send_ref):
    mine = lax.rem(lax.axis_index("dp"), 2)
    for z in range(QUERY_HEADS // 2):
        to = slice(z * HEAD_WIDTH, (z + 1) * HEAD_WIDTH)
        keep = pl.multiple_of((2 * z + mine) * HEAD_WIDTH, HEAD_WIDTH)
        send = pl.multiple_of((2 * z + 1 - mine) * HEAD_WIDTH, HEAD_WIDTH)
        keep_ref[to, :] = att_ref[pl.ds(keep, HEAD_WIDTH), :]
        send_ref[to, :] = att_ref[pl.ds(send, HEAD_WIDTH), :]


def weight_part_body(parts, keep_ref, other_ref, dy_ref, dy_other_ref, *outs):
    me = lax.axis_index("ctx")
    cols = dy_ref.shape[1] // parts
    left = jnp.concatenate([keep_ref[...], other_ref[...]], 1)
    for m, out in enumerate(outs):
        at = pl.ds(pl.multiple_of((me ^ m) * cols, cols), cols)
        right = jnp.concatenate([dy_ref[:, at], dy_other_ref[:, at]], 0)
        out[...] = dot(left, right, NN).astype(out.dtype)


def weight_plane_body(count, *refs):
    ins, outs = refs[:count], refs[count:]
    me = lax.axis_index("dp") // 2
    rows = outs[0].shape[0]
    for m, out in enumerate(outs):
        at = pl.ds(pl.multiple_of(lax.rem(me + m, len(outs)) * rows, rows), rows)
        total = ins[0][at, :].astype(F32)
        for r in ins[1:]:
            total = total + r[at, :].astype(F32)
        out[...] = total.astype(out.dtype)


def weight_sum_body(factor, *refs):
    total = refs[0][...].astype(F32)
    for r in refs[1:-1]:
        total = total + r[...].astype(F32)
    refs[-1][...] = total * factor


def head_at(h):
    start = h * HEAD_WIDTH
    return pl.ds(start if isinstance(h, int) else pl.multiple_of(start, HEAD_WIDTH), HEAD_WIDTH)


def lanes_at(start):
    return pl.ds(start if isinstance(start, int) else pl.multiple_of(start, HEAD_WIDTH), HEAD_WIDTH)


def band_of(refs, tokens, start):
    return jnp.concatenate([r[:tokens, lanes_at(start)] for r in refs], 0)


def heads_backward(heads, group, q_ref, band, dy_ref, prob_ref, attf_ref, pieces, ds_ref, first):
    tokens = q_ref.shape[0]
    width = band[0].shape[1] // 2
    values = band_of(band, tokens, width + group * HEAD_WIDTH)
    probs, d_rows, q_rows = [], [], []
    for i, (h, piece) in enumerate(zip(heads, pieces)):
        at = head_at(h)
        dat = dot(piece[...], dy_ref[...], NT).astype(BF16)
        delta = (dat.astype(F32) * attf_ref[at, :]).sum(axis=0, keepdims=True)
        prob = prob_ref[:, at]
        ds_ref[:, head_at(first + i)] = (prob.astype(F32) * (dot(values, dat, NN) - delta)).astype(BF16)
        probs.append(prob)
        d_rows.append(dat.T)
        q_rows.append(q_ref[:, at])
    ds = ds_ref[:, first * HEAD_WIDTH : (first + len(heads)) * HEAD_WIDTH]
    part_k = dot(ds, jnp.concatenate(q_rows, 0), NN)
    part_v = dot(jnp.concatenate(probs, 1), jnp.concatenate(d_rows, 0), NN)
    return part_k, part_v


def backward_first_body(scale, place, q_ref, prev_ref, own_ref, next_ref, dy_ref, prob_ref, attf_ref, *rest):
    pieces, (whole_ref, half_ref, ds_ref) = rest[:6], rest[6:]
    head, group = place()
    band = (prev_ref, own_ref, next_ref)
    shared = (q_ref, band, dy_ref, prob_ref, attf_ref)
    part_k, part_v = heads_backward([head(j) for j in range(4)], group(0), *shared, pieces[:4], ds_ref, 0)
    whole_ref[:, :HEAD_WIDTH] = (part_k * scale).astype(BF16)
    whole_ref[:, HEAD_WIDTH:] = part_v.astype(BF16)
    part_k, part_v = heads_backward([head(j) for j in (4, 5)], group(4), *shared, pieces[4:], ds_ref, 4)
    half_ref[:, :HEAD_WIDTH] = part_k
    half_ref[:, HEAD_WIDTH:] = part_v


def backward_second_body(scale, place, q_ref, prev_ref, own_ref, next_ref, dy_ref, prob_ref, attf_ref, *rest):
    pieces, whole_ref, half_ref = rest[:2], rest[2], rest[3]
    outs, ds_ref = rest[4:7], rest[7]
    head, group = place()
    tokens = q_ref.shape[0]
    width = own_ref.shape[1] // 2
    band = (prev_ref, own_ref, next_ref)
    shared = (q_ref, band, dy_ref, prob_ref, attf_ref)
    part_k, part_v = heads_backward([head(j) for j in (6, 7)], group(6), *shared, pieces, ds_ref, 0)
    part_k = ((part_k + half_ref[:, :HEAD_WIDTH]) * scale).astype(BF16)
    part_v = (part_v + half_ref[:, HEAD_WIDTH:]).astype(BF16)
    for t, out in enumerate(outs):
        rows = slice(t * tokens, (t + 1) * tokens)
        out[:, lanes_at(group(6) * HEAD_WIDTH)] = part_k[rows]
        out[:, lanes_at(width + group(6) * HEAD_WIDTH)] = part_v[rows]
        out[:, lanes_at(group(0) * HEAD_WIDTH)] = whole_ref[rows, :HEAD_WIDTH]
        out[:, lanes_at(width + group(0) * HEAD_WIDTH)] = whole_ref[rows, HEAD_WIDTH:]


def output_body(scale, place, prev_ref, own_ref, next_ref, ds_ref, ds_last_ref, att_ref, *rest):
    pieces, (mixed_ref, gq_ref) = rest[:QUERY_HEADS], rest[QUERY_HEADS:]
    head, group = place()
    tokens = mixed_ref.shape[0]
    ds = (ds_ref[:, : 4 * HEAD_WIDTH], jnp.concatenate([ds_ref[:, 4 * HEAD_WIDTH :], ds_last_ref[...]], 1))
    for half in range(2):
        keys = band_of((prev_ref, own_ref, next_ref), tokens, group(4 * half) * HEAD_WIDTH)
        dq = dot(keys.T, ds[half], NN) * scale
        for i in range(4):
            gq_ref[:, head_at(head(4 * half + i))] = dq[:, i * tokens : (i + 1) * tokens].T.astype(BF16)
    total = jnp.zeros(mixed_ref.shape, F32)
    for j in range(0, QUERY_HEADS, 2):
        att = jnp.concatenate([att_ref[head_at(head(i)), :].T for i in (j, j + 1)], 1)
        total = total + dot(att, jnp.concatenate([pieces[j][...], pieces[j + 1][...]], 0), NN)
    mixed_ref[...] = total.astype(BF16)


def key_value_body(own_ref, low_ref, high_ref, gk_ref, gv_ref):
    width = gk_ref.shape[1]
    total = own_ref[...].astype(F32) + low_ref[...].astype(F32) + high_ref[...].astype(F32)
    gk_ref[...] = total[:, :width].astype(BF16)
    gv_ref[...] = total[:, width:].astype(BF16)


def power_of_two(n):
    return n & (n - 1) == 0


def flip(value, axis, mask):
    return lax.ppermute(value, axis, [(i, i ^ mask) for i in range(lax.axis_size(axis))])


def turn(value, axis, step):
    count = lax.axis_size(axis)
    return lax.ppermute(value, axis, [(i, (i + step) % count) for i in range(count)])


def sublayer(queries, keys_in, values_in, patch_order, block_mask, out_weight, cotangent):
    scale = 1.0 / math.sqrt(HEAD_WIDTH)
    n_dp, n_ctx = lax.axis_size("dp"), lax.axis_size("ctx")
    q, k, v, dy = queries[0], keys_in[0], values_in[0], cotangent[0]
    tokens, query_width = q.shape
    kv_width = k.shape[1]
    model = dy.shape[1]
    band = 3 * tokens
    by_head = n_dp == QUERY_HEADS
    column_width = model // n_ctx
    staged = by_head and power_of_two(n_ctx) and column_width % 128 == 0
    macs = tokens * query_width
    group_heads = QUERY_HEADS // KEY_VALUE_HEADS

    own = call(
        pack_body,
        [shape((tokens + HALO_ROWS, 2 * kv_width))],
        [hbm()] * 3,
        in_hbm(k, v, patch_order[0]),
        scratch=[pltpu.VMEM((1, tokens), jnp.int32), pltpu.SemaphoreType.DMA((3,))],
        room=16<<20,
    )[0]
    dy_hbm = dy
    q, dy = call(
        fetch_body, [shape(q.shape), shape(dy.shape)], [hbm()] * 2, in_hbm(q, dy),
        scratch=[pltpu.SemaphoreType.DMA((2,))],
    )
    prev_kv = turn(own, "ctx", 1)
    next_kv = turn(own, "ctx", -1)

    if by_head:
        mine = {0: out_weight}
        for j in range(n_dp // 2, 1, -2):
            mine[j] = flip(out_weight, "dp", j)
        for j in range(n_dp // 2 + 2, n_dp, 2):
            mine[j] = flip(mine[n_dp // 2], "dp", j - n_dp // 2)

        def place():
            me = lax.axis_index("dp")
            return (lambda j: me ^ j), (lambda j: (me ^ j) // group_heads)
    else:
        weight_all = lax.all_gather(out_weight, "dp", axis=0, tiled=True)
        pieces = [weight_all.reshape(QUERY_HEADS, HEAD_WIDTH, model)[h] for h in range(QUERY_HEADS)]

        def place():
            return (lambda j: j), (lambda j: j // group_heads)

    prob, attf, att = call(
        functools.partial(forward_body, scale),
        [shape((band, query_width)), shape((query_width, tokens), F32), shape((query_width, tokens))],
        [vmem()] * 4 + [smem()],
        (q, prev_kv, own, next_kv, block_mask[0]),
        flops=4 * macs * band,
    )

    total_tokens = n_dp * tokens * n_ctx
    norm_factor = 1.0 / math.sqrt(total_tokens)
    if staged:
        dy_other = flip(dy_hbm, "dp", 1)
        half = query_width // 2
        keep, send = call(split_body, [shape((half, tokens))] * 2, [vmem()], (att,))
        other = flip(send, "dp", 1)
        parts = call(
            functools.partial(weight_part_body, n_ctx),
            [shape((half, column_width))] * n_ctx,
            [vmem()] * 4,
            (keep, other, dy, dy_other),
            flops=2 * half * 2 * tokens * model,
        )
        arrived = [parts[0]]
        for m in range(1, n_ctx):
            arrived.append(flip(parts[m], "ctx", m))
        n_z = n_dp // 2
        blocks = call(
            functools.partial(weight_plane_body, n_ctx),
            [shape((half // n_z, column_width))] * n_z,
            [vmem()] * n_ctx,
            arrived,
        )
        landed = [blocks[0]]
        for m in range(1, n_z):
            landed.append(turn(blocks[m], "dp", 2 * m))
        grad_weight = call(
            functools.partial(weight_sum_body, norm_factor),
            [shape((half // n_z, column_width), F32)],
            [vmem()] * n_z,
            landed,
        )[0]
    else:
        part = dot(att, dy, NN).astype(BF16)
        columns = lax.psum_scatter(part, "ctx", scatter_dimension=1, tiled=True).astype(F32)
        grad_weight = lax.psum_scatter(columns, "dp", scatter_dimension=0, tiled=True) * norm_factor

    if by_head:
        pieces = []
        for j in range(0, n_dp, 2):
            pieces += [mine[j], flip(mine[j], "dp", 1)]

    whole, half_sum, ds = call(
        functools.partial(backward_first_body, scale, place),
        [shape((band, 2 * HEAD_WIDTH)), shape((band, 2 * HEAD_WIDTH), F32), shape((band, 6 * HEAD_WIDTH))],
        [vmem()] * 13,
        (q, prev_kv, own, next_kv, dy, prob, attf, *pieces[:6]),
        flops=(2 * macs * model + 6 * macs * band) * 3 // 4,
    )
    low, mid, high, ds_last = call(
        functools.partial(backward_second_body, scale, place),
        [shape((tokens, 2 * kv_width))] * 3 + [shape((band, 2 * HEAD_WIDTH))],
        [vmem()] * 11,
        (q, prev_kv, own, next_kv, dy, prob, attf, *pieces[6:], whole, half_sum),
        flops=(2 * macs * model + 6 * macs * band) // 4,
    )
    from_next = turn(low, "ctx", -1)
    from_prev = turn(high, "ctx", 1)
    mixed, grad_q = call(
        functools.partial(output_body, scale, place),
        [shape((tokens, model)), shape((tokens, query_width))],
        [vmem()] * 14,
        (prev_kv, own, next_kv, ds, ds_last, att, *pieces),
        flops=2 * macs * model + 2 * macs * band,
    )
    grad_k, grad_v = call(key_value_body, [shape((tokens, kv_width))] * 2, [vmem()] * 3, (mid, from_next, from_prev))
    return (mixed[None], grad_q[None], grad_k[None], grad_v[None], grad_weight)


def solution(mesh):
    row = P("dp", "ctx", None)
    in_specs = (row, row, row, row, row, P("dp", None), row)
    out_specs = (row, row, row, row, P("dp", "ctx"))
    return jax.shard_map(sublayer, mesh=mesh, in_specs=in_specs, out_specs=out_specs, check_vma=False)
```

profile of v0, /device:TPU:0, one launch (start us, length us, event | category | flops | bytes accessed | tf_op | source)
XLA Modules:
  0.0 53.0 jit_solution(8561581473284876418)
XLA Ops:
  0.6 0.0 copy-start
  0.6 4.1 %collective-permute-start.5 = (bf16[128,1024]{1,0:T(8,128)(2,1)}, bf16[128,1024]{1,0:T(8,128)(2,1)S(1)}, u32[]{:S(2)}, u32[]{:S(2)}) collective-permute-start(bf16[128,1024]{1,0:T(8,128)(2,1)} %rest_0_.3), channel_id=1, source_target_pairs={{0,4},{1,5},{2,6},{3,7},{4,0},{5,1},{6,2},{7,3},{8,12},{9,13},{10,... | collective-permute-start | bytes 786440 | tf_op jit(solution)/shard_map/ppermute | solution.py:268
  4.8 1.6 %collective-permute-start.3 = (bf16[128,1024]{1,0:T(8,128)(2,1)}, bf16[128,1024]{1,0:T(8,128)(2,1)S(1)}, u32[]{:S(2)}, u32[]{:S(2)}) collective-permute-start(bf16[128,1024]{1,0:T(8,128)(2,1)} %rest_0_.3), channel_id=1, source_target_pairs={{0,2},{1,3},{2,0},{3,1},{4,6},{5,7},{6,4},{7,5},{8,10},{9,11},{10,... | collective-permute-start | bytes 786440 | tf_op jit(solution)/shard_map/ppermute | solution.py:268
  6.3 0.9 %shard_map.110.own_ref = bf16[136,512]{1,0:T(8,128)(2,1)S(1)} custom-call(bf16[128,256]{1,0:T(8,128)(2,1)} %bitcast.14, bf16[128,256]{1,0:T(8,128)(2,1)} %bitcast.15, s32[1,128]{1,0:T(1,128)} %bitcast.16), custom_call_target="tpu_custom_call" | custom-call | flops 1048576 | bytes 270848 | tf_op jit(solution)/shard_map/pallas_call | solution.py:47
  7.3 1.5 %collective-permute-start = (bf16[136,512]{1,0:T(8,128)(2,1)S(1)}, bf16[136,512]{1,0:T(8,128)(2,1)S(1)}, u32[]{:S(2)}, u32[]{:S(2)}) collective-permute-start(bf16[136,512]{1,0:T(8,128)(2,1)S(1)} %shard_map.110.own_ref), channel_id=1, source_target_pairs={{0,8},{8,16},{16,24},{24,0},{1,9},{9,17},{17,25},{25,1},{2,10},{10... | collective-permute-start | bytes 417800 | tf_op jit(solution)/shard_map/ppermute | solution.py:273
  8.8 0.0 collective-permute-start.12
  8.8 1.4 %collective-permute-start.1 = (bf16[136,512]{1,0:T(8,128)(2,1)S(1)}, bf16[136,512]{1,0:T(8,128)(2,1)S(1)}, u32[]{:S(2)}, u32[]{:S(2)}) collective-permute-start(bf16[136,512]{1,0:T(8,128)(2,1)S(1)} %shard_map.110.own_ref), channel_id=1, source_target_pairs={{0,24},{8,0},{16,8},{24,16},{1,25},{9,1},{17,9},{25,17},{2,26},{10... | collective-permute-start | bytes 417800 | tf_op jit(solution)/shard_map/ppermute | solution.py:273
  10.2 6.8 %collective-permute-done.5.rest_4_ = bf16[128,1024]{1,0:T(8,128)(2,1)S(1)} collective-permute-done((bf16[128,1024]{1,0:T(8,128)(2,1)}, bf16[128,1024]{1,0:T(8,128)(2,1)S(1)}, u32[]{:S(2)}, u32[]{:S(2)}) %collective-permute-start.5) | collective-permute-done | bytes 262176 | tf_op jit(solution)/shard_map/ppermute | solution.py:268
  17.0 0.7 %collective-permute-start.7 = (bf16[128,1024]{1,0:T(8,128)(2,1)S(1)}, bf16[128,1024]{1,0:T(8,128)(2,1)S(1)}, u32[]{:S(2)}, u32[]{:S(2)}) collective-permute-start(bf16[128,1024]{1,0:T(8,128)(2,1)S(1)} %collective-permute-done.5.rest_4_), channel_id=1, source_target_pairs={{0,2},{1,3},{2,0},{3,1},{4,6},{5,7},{6,4},{7,5},{8,10},{9,11},{10,... | collective-permute-start | bytes 786440 | tf_op jit(solution)/shard_map/ppermute | solution.py:268
  17.7 0.0 collective-permute-done.prev_ref
  17.7 0.0 copy-done
  17.7 0.0 collective-permute-start.2
  17.7 0.0 collective-permute-done.3.rest_2_
  17.8 0.5 collective-permute-start.4
  18.3 1.0 %shard_map.111 = (bf16[128,1024]{1,0:T(8,128)(2,1)S(1)}, bf16[128,1024]{1,0:T(8,128)(2,1)S(1)}) custom-call(bf16[128,1024]{1,0:T(8,128)(2,1)} %bitcast.11, bf16[128,1024]{1,0:T(8,128)(2,1)} %bitcast.13), custom_call_target="tpu_custom_call" | custom-call | flops 1048576 | bytes 1048576 | tf_op jit(solution)/shard_map/pallas_call | solution.py:47
  19.3 0.0 copy-start.1
  19.3 0.0 collective-permute-done.1.next_ref
  19.3 0.7 %copy-done.1 = s32[1,4,8]{2,1,0:T(4,128)S(1)} copy-done((s32[1,4,8]{2,1,0:T(4,128)S(1)}, s32[1,4,8]{2,1,0:T(4,128)}, u32[]{:S(2)}) %copy-start.1) | copy-done | bytes 152
  20.0 1.7 %shard_map.112 = (bf16[384,1024]{1,0:T(8,128)(2,1)S(1)}, f32[1024,128]{1,0:T(8,128)S(1)}, bf16[1024,128]{1,0:T(8,128)(2,1)S(1)}) custom-call(bf16[128,1024]{1,0:T(8,128)(2,1)S(1)} %get-tuple-element.31.q_ref, bf16[136,512]{1,0:T(8,128)(2,1)S(1)} %collective-permute-done.prev_ref, bf16[136,512]{1,0:T(8,128)(2,1)S(1)} %shard_map.110.own_ref, ...), custom_call_target="tpu_custom_call" | custom-call | flops 201326592 | bytes 2252928 | tf_op jit(solution)/shard_map/pallas_call | solution.py:47
  21.7 0.1 collective-permute-start.11
  21.9 0.0 collective-permute-done.12.dy_other_ref
  21.9 0.4 collective-permute-start.6
  22.3 2.1 %collective-permute-done.7.rest_0_.rest_6_ = bf16[128,1024]{1,0:T(8,128)(2,1)S(1)} collective-permute-done((bf16[128,1024]{1,0:T(8,128)(2,1)S(1)}, bf16[128,1024]{1,0:T(8,128)(2,1)S(1)}, u32[]{:S(2)}, u32[]{:S(2)}) %collective-permute-start.7) | collective-permute-done | bytes 262176 | tf_op jit(solution)/shard_map/ppermute | solution.py:268
  24.4 0.0 collective-permute-start.8
  24.4 0.0 collective-permute-done.11.other_ref
  24.4 0.5 shard_map.118
  24.9 1.4 %collective-permute-start.13 = (bf16[512,256]{1,0:T(8,128)(2,1)S(1)}, bf16[512,256]{1,0:T(8,128)(2,1)S(1)}, u32[]{:S(2)}, u32[]{:S(2)}) collective-permute-start(bf16[512,256]{1,0:T(8,128)(2,1)S(1)} %get-tuple-element.50), channel_id=1, source_target_pairs={{0,8},{8,0},{16,24},{24,16},{1,9},{9,1},{17,25},{25,17},{2,10},{10... | collective-permute-start | bytes 786440 | tf_op jit(solution)/shard_map/ppermute | solution.py:268
  26.2 0.0 collective-permute-done.2.rest_1_
  26.2 1.5 %collective-permute-start.14 = (bf16[512,256]{1,0:T(8,128)(2,1)S(1)}, bf16[512,256]{1,0:T(8,128)(2,1)S(1)}, u32[]{:S(2)}, u32[]{:S(2)}) collective-permute-start(bf16[512,256]{1,0:T(8,128)(2,1)S(1)} %get-tuple-element.51), channel_id=1, source_target_pairs={{0,16},{8,24},{16,0},{24,8},{1,17},{9,25},{17,1},{25,9},{2,18},{10... | collective-permute-start | bytes 786440 | tf_op jit(solution)/shard_map/ppermute | solution.py:268
  27.8 0.0 collective-permute-done.4.rest_3_
  27.8 0.7 %collective-permute-start.15 = (bf16[512,256]{1,0:T(8,128)(2,1)S(1)}, bf16[512,256]{1,0:T(8,128)(2,1)S(1)}, u32[]{:S(2)}, u32[]{:S(2)}) collective-permute-start(bf16[512,256]{1,0:T(8,128)(2,1)S(1)} %get-tuple-element.52), channel_id=1, source_target_pairs={{0,24},{8,16},{16,8},{24,0},{1,25},{9,17},{17,9},{25,1},{2,26},{10... | collective-permute-start | bytes 786440 | tf_op jit(solution)/shard_map/ppermute | solution.py:268
  28.5 0.0 collective-permute-done.6.rest_5_
  28.5 2.2 %shard_map.113 = (bf16[384,256]{1,0:T(8,128)(2,1)S(1)}, f32[384,256]{1,0:T(8,128)S(1)}, bf16[384,768]{1,0:T(8,128)(2,1)S(1)}) custom-call(bf16[128,1024]{1,0:T(8,128)(2,1)S(1)} %get-tuple-element.31.q_ref, bf16[136,512]{1,0:T(8,128)(2,1)S(1)} %collective-permute-done.prev_ref, bf16[136,512]{1,0:T(8,128)(2,1)S(1)} %shard_map.110.own_ref, ...), custom_call_target="tpu_custom_call" | custom-call | flops 427819008 | bytes 5005312 | tf_op jit(solution)/shard_map/pallas_call | solution.py:47
  30.7 0.0 collective-permute-done.8.rest_1_.rest_7_
  30.7 1.0 %shard_map.114 = (bf16[128,512]{1,0:T(8,128)(2,1)S(1)}, bf16[128,512]{1,0:T(8,128)(2,1)S(1)}, bf16[128,512]{1,0:T(8,128)(2,1)S(1)}, bf16[384,256]{1,0:T(8,128)(2,1)S(1)}) custom-call(bf16[128,1024]{1,0:T(8,128)(2,1)S(1)} %get-tuple-element.31.q_ref, bf16[136,512]{1,0:T(8,128)(2,1)S(1)} %collective-permute-done.prev_ref, ...), custom_call_target="tpu_custom_call" | custom-call | flops 142606336 | bytes 3956736 | tf_op jit(solution)/shard_map/pallas_call | solution.py:47
  31.7 2.3 %collective-permute-start.9 = (bf16[128,512]{1,0:T(8,128)(2,1)S(1)}, bf16[128,512]{1,0:T(8,128)(2,1)S(1)}, u32[]{:S(2)}, u32[]{:S(2)}) collective-permute-start(bf16[128,512]{1,0:T(8,128)(2,1)S(1)} %get-tuple-element.43), channel_id=1, source_target_pairs={{0,24},{8,0},{16,8},{24,16},{1,25},{9,1},{17,9},{25,17},{2,26},{10... | collective-permute-start | bytes 393224 | tf_op jit(solution)/shard_map/ppermute | solution.py:273
  34.0 0.0 collective-permute-start.10
  34.0 0.2 collective-permute-done.13.refs_1_
  34.1 5.9 %collective-permute-done.14.refs_2_ = bf16[512,256]{1,0:T(8,128)(2,1)S(1)} collective-permute-done((bf16[512,256]{1,0:T(8,128)(2,1)S(1)}, bf16[512,256]{1,0:T(8,128)(2,1)S(1)}, u32[]{:S(2)}, u32[]{:S(2)}) %collective-permute-start.14) | collective-permute-done | bytes 262176 | tf_op jit(solution)/shard_map/ppermute | solution.py:268
  40.1 0.5 collective-permute-done.15.refs_3_
  40.5 0.1 shard_map.119
  40.7 1.8 %collective-permute-start.16 = (bf16[128,256]{1,0:T(8,128)(2,1)S(1)}, bf16[128,256]{1,0:T(8,128)(2,1)S(1)}, u32[]{:S(2)}, u32[]{:S(2)}) collective-permute-start(bf16[128,256]{1,0:T(8,128)(2,1)S(1)} %get-tuple-element.54), channel_id=1, source_target_pairs={{0,2},{1,3},{2,4},{3,5},{4,6},{5,7},{6,0},{7,1},{8,10},{9,11},{10,... | collective-permute-start | bytes 196616 | tf_op jit(solution)/shard_map/ppermute | solution.py:273
  42.5 3.3 %collective-permute-start.17 = (bf16[128,256]{1,0:T(8,128)(2,1)S(1)}, bf16[128,256]{1,0:T(8,128)(2,1)S(1)}, u32[]{:S(2)}, u32[]{:S(2)}) collective-permute-start(bf16[128,256]{1,0:T(8,128)(2,1)S(1)} %get-tuple-element.55), channel_id=1, source_target_pairs={{0,4},{1,5},{2,6},{3,7},{4,0},{5,1},{6,2},{7,3},{8,12},{9,13},{10,... | collective-permute-start | bytes 196616 | tf_op jit(solution)/shard_map/ppermute | solution.py:273
  45.7 1.2 %collective-permute-start.18 = (bf16[128,256]{1,0:T(8,128)(2,1)S(1)}, bf16[128,256]{1,0:T(8,128)(2,1)S(1)}, u32[]{:S(2)}, u32[]{:S(2)}) collective-permute-start(bf16[128,256]{1,0:T(8,128)(2,1)S(1)} %get-tuple-element.56), channel_id=1, source_target_pairs={{0,6},{1,7},{2,0},{3,1},{4,2},{5,3},{6,4},{7,5},{8,14},{9,15},{10,... | collective-permute-start | bytes 196616 | tf_op jit(solution)/shard_map/ppermute | solution.py:273
  46.9 1.3 %collective-permute-done.16.refs_1_ = bf16[128,256]{1,0:T(8,128)(2,1)S(1)} collective-permute-done((bf16[128,256]{1,0:T(8,128)(2,1)S(1)}, bf16[128,256]{1,0:T(8,128)(2,1)S(1)}, u32[]{:S(2)}, u32[]{:S(2)}) %collective-permute-start.16) | collective-permute-done | bytes 65568 | tf_op jit(solution)/shard_map/ppermute | solution.py:273
  48.2 1.7 %collective-permute-done.17.refs_2_ = bf16[128,256]{1,0:T(8,128)(2,1)S(1)} collective-permute-done((bf16[128,256]{1,0:T(8,128)(2,1)S(1)}, bf16[128,256]{1,0:T(8,128)(2,1)S(1)}, u32[]{:S(2)}, u32[]{:S(2)}) %collective-permute-start.17) | collective-permute-done | bytes 65568 | tf_op jit(solution)/shard_map/ppermute | solution.py:273
  49.9 0.4 collective-permute-done.18.refs_3_
  50.3 0.7 %shard_map.120 = f32[128,256]{1,0:T(8,128)} custom-call(bf16[128,256]{1,0:T(8,128)(2,1)S(1)} %get-tuple-element.53.refs_0_, bf16[128,256]{1,0:T(8,128)(2,1)S(1)} %collective-permute-done.16.refs_1_, bf16[128,256]{1,0:T(8,128)(2,1)S(1)} %collective-permute-done.17.refs_2_, bf16[128,256]{1,0:T(8,128)(2,1)S(1)} %collective-permute-done.18.refs_3_), custom_call_target="tpu_custom_call" | custom-call | flops 1048576 | bytes 393216 | tf_op jit(solution)/shard_map/pallas_call | solution.py:47
  51.0 1.4 %shard_map.115 = (bf16[128,1024]{1,0:T(8,128)(2,1)}, bf16[128,1024]{1,0:T(8,128)(2,1)}) custom-call(bf16[136,512]{1,0:T(8,128)(2,1)S(1)} %collective-permute-done.prev_ref, bf16[136,512]{1,0:T(8,128)(2,1)S(1)} %shard_map.110.own_ref, bf16[136,512]{1,0:T(8,128)(2,1)S(1)} %collective-permute-done.1.next_ref, bf16[384,768]{1,0:T(8,128)(2,1)S(1)} %get-tuple-element.35.ds_ref, ...), custom_call_target="tpu_custom_call" | custom-call | flops 369098752 | bytes 4087808 | tf_op jit(solution)/shard_map/pallas_call | solution.py:47
  52.4 0.0 collective-permute-done.9.low_ref
  52.4 0.0 collective-permute-done.10.high_ref
  52.4 0.7 %shard_map.116 = (bf16[128,256]{1,0:T(8,128)(2,1)}, bf16[128,256]{1,0:T(8,128)(2,1)}) custom-call(bf16[128,512]{1,0:T(8,128)(2,1)S(1)} %get-tuple-element.42.own_ref, bf16[128,512]{1,0:T(8,128)(2,1)S(1)} %collective-permute-done.9.low_ref, bf16[128,512]{1,0:T(8,128)(2,1)S(1)} %collective-permute-done.10.high_ref), custom_call_target="tpu_custom_call" | custom-call | flops 1048576 | bytes 524288 | tf_op jit(solution)/shard_map/pallas_call | solution.py:47
  (1 shorter events, 0.0 us)
Async XLA Ops:
  0.6 17.1 %copy-start = (bf16[128,1024]{1,0:T(8,128)(2,1)S(1)}, bf16[128,1024]{1,0:T(8,128)(2,1)}, u32[]{:S(2)}) copy-start(bf16[128,1024]{1,0:T(8,128)(2,1)} %rest_0_.3) | copy-start | bytes 786436
  0.6 16.4 %collective-permute-start.5 = (bf16[128,1024]{1,0:T(8,128)(2,1)}, bf16[128,1024]{1,0:T(8,128)(2,1)S(1)}, u32[]{:S(2)}, u32[]{:S(2)}) collective-permute-start(bf16[128,1024]{1,0:T(8,128)(2,1)} %rest_0_.3), channel_id=1, source_target_pairs={{0,4},{1,5},{2,6},{3,7},{4,0},{5,1},{6,2},{7,3},{8,12},{9,13},{10,... | collective-permute-start | bytes 786440 | tf_op jit(solution)/shard_map/ppermute | solution.py:268
  4.8 13.0 %collective-permute-start.3 = (bf16[128,1024]{1,0:T(8,128)(2,1)}, bf16[128,1024]{1,0:T(8,128)(2,1)S(1)}, u32[]{:S(2)}, u32[]{:S(2)}) collective-permute-start(bf16[128,1024]{1,0:T(8,128)(2,1)} %rest_0_.3), channel_id=1, source_target_pairs={{0,2},{1,3},{2,0},{3,1},{4,6},{5,7},{6,4},{7,5},{8,10},{9,11},{10,... | collective-permute-start | bytes 786440 | tf_op jit(solution)/shard_map/ppermute | solution.py:268
  7.3 10.5 %collective-permute-start = (bf16[136,512]{1,0:T(8,128)(2,1)S(1)}, bf16[136,512]{1,0:T(8,128)(2,1)S(1)}, u32[]{:S(2)}, u32[]{:S(2)}) collective-permute-start(bf16[136,512]{1,0:T(8,128)(2,1)S(1)} %shard_map.110.own_ref), channel_id=1, source_target_pairs={{0,8},{8,16},{16,24},{24,0},{1,9},{9,17},{17,25},{25,1},{2,10},{10... | collective-permute-start | bytes 417800 | tf_op jit(solution)/shard_map/ppermute | solution.py:273
  8.8 13.1 %collective-permute-start.12 = (bf16[128,1024]{1,0:T(8,128)(2,1)}, bf16[128,1024]{1,0:T(8,128)(2,1)S(1)}, u32[]{:S(2)}, u32[]{:S(2)}) collective-permute-start(bf16[128,1024]{1,0:T(8,128)(2,1)} %bitcast.12), channel_id=1, source_target_pairs={{0,1},{1,0},{2,3},{3,2},{4,5},{5,4},{6,7},{7,6},{8,9},{9,8},{10,11... | collective-permute-start | bytes 786440 | tf_op jit(solution)/shard_map/ppermute | solution.py:268
  8.8 10.5 %collective-permute-start.1 = (bf16[136,512]{1,0:T(8,128)(2,1)S(1)}, bf16[136,512]{1,0:T(8,128)(2,1)S(1)}, u32[]{:S(2)}, u32[]{:S(2)}) collective-permute-start(bf16[136,512]{1,0:T(8,128)(2,1)S(1)} %shard_map.110.own_ref), channel_id=1, source_target_pairs={{0,24},{8,0},{16,8},{24,16},{1,25},{9,1},{17,9},{25,17},{2,26},{10... | collective-permute-start | bytes 417800 | tf_op jit(solution)/shard_map/ppermute | solution.py:273
  17.0 7.4 %collective-permute-start.7 = (bf16[128,1024]{1,0:T(8,128)(2,1)S(1)}, bf16[128,1024]{1,0:T(8,128)(2,1)S(1)}, u32[]{:S(2)}, u32[]{:S(2)}) collective-permute-start(bf16[128,1024]{1,0:T(8,128)(2,1)S(1)} %collective-permute-done.5.rest_4_), channel_id=1, source_target_pairs={{0,2},{1,3},{2,0},{3,1},{4,6},{5,7},{6,4},{7,5},{8,10},{9,11},{10,... | collective-permute-start | bytes 786440 | tf_op jit(solution)/shard_map/ppermute | solution.py:268
  17.7 8.5 %collective-permute-start.2 = (bf16[128,1024]{1,0:T(8,128)(2,1)S(1)}, bf16[128,1024]{1,0:T(8,128)(2,1)S(1)}, u32[]{:S(2)}, u32[]{:S(2)}) collective-permute-start(bf16[128,1024]{1,0:T(8,128)(2,1)S(1)} %copy-done), channel_id=1, source_target_pairs={{0,1},{1,0},{2,3},{3,2},{4,5},{5,4},{6,7},{7,6},{8,9},{9,8},{10,11... | collective-permute-start | bytes 786440 | tf_op jit(solution)/shard_map/ppermute | solution.py:268
  17.8 10.0 %collective-permute-start.4 = (bf16[128,1024]{1,0:T(8,128)(2,1)S(1)}, bf16[128,1024]{1,0:T(8,128)(2,1)S(1)}, u32[]{:S(2)}, u32[]{:S(2)}) collective-permute-start(bf16[128,1024]{1,0:T(8,128)(2,1)S(1)} %collective-permute-done.3.rest_2_), channel_id=1, source_target_pairs={{0,1},{1,0},{2,3},{3,2},{4,5},{5,4},{6,7},{7,6},{8,9},{9,8},{10,11... | collective-permute-start | bytes 786440 | tf_op jit(solution)/shard_map/ppermute | solution.py:268
  19.3 0.7 %copy-start.1 = (s32[1,4,8]{2,1,0:T(4,128)S(1)}, s32[1,4,8]{2,1,0:T(4,128)}, u32[]{:S(2)}) copy-start(s32[1,4,8]{2,1,0:T(4,128)} %param.11) | copy-start | bytes 388
  21.7 2.7 %collective-permute-start.11 = (bf16[512,128]{1,0:T(8,128)(2,1)S(1)}, bf16[512,128]{1,0:T(8,128)(2,1)S(1)}, u32[]{:S(2)}, u32[]{:S(2)}) collective-permute-start(bf16[512,128]{1,0:T(8,128)(2,1)S(1)} %get-tuple-element.48), channel_id=1, source_target_pairs={{0,1},{1,0},{2,3},{3,2},{4,5},{5,4},{6,7},{7,6},{8,9},{9,8},{10,11... | collective-permute-start | bytes 393224 | tf_op jit(solution)/shard_map/ppermute | solution.py:268
  21.9 6.6 %collective-permute-start.6 = (bf16[128,1024]{1,0:T(8,128)(2,1)S(1)}, bf16[128,1024]{1,0:T(8,128)(2,1)S(1)}, u32[]{:S(2)}, u32[]{:S(2)}) collective-permute-start(bf16[128,1024]{1,0:T(8,128)(2,1)S(1)} %collective-permute-done.5.rest_4_), channel_id=1, source_target_pairs={{0,1},{1,0},{2,3},{3,2},{4,5},{5,4},{6,7},{7,6},{8,9},{9,8},{10,11... | collective-permute-start | bytes 786440 | tf_op jit(solution)/shard_map/ppermute | solution.py:268
  24.4 6.3 %collective-permute-start.8 = (bf16[128,1024]{1,0:T(8,128)(2,1)S(1)}, bf16[128,1024]{1,0:T(8,128)(2,1)S(1)}, u32[]{:S(2)}, u32[]{:S(2)}) collective-permute-start(bf16[128,1024]{1,0:T(8,128)(2,1)S(1)} %collective-permute-done.7.rest_0_.rest_6_), channel_id=1, source_target_pairs={{0,1},{1,0},{2,3},{3,2},{4,5},{5,4},{6,7},{7,6},{8,9},{9,8},{10,11... | collective-permute-start | bytes 786440 | tf_op jit(solution)/shard_map/ppermute | solution.py:268
  24.9 9.2 %collective-permute-start.13 = (bf16[512,256]{1,0:T(8,128)(2,1)S(1)}, bf16[512,256]{1,0:T(8,128)(2,1)S(1)}, u32[]{:S(2)}, u32[]{:S(2)}) collective-permute-start(bf16[512,256]{1,0:T(8,128)(2,1)S(1)} %get-tuple-element.50), channel_id=1, source_target_pairs={{0,8},{8,0},{16,24},{24,16},{1,9},{9,1},{17,25},{25,17},{2,10},{10... | collective-permute-start | bytes 786440 | tf_op jit(solution)/shard_map/ppermute | solution.py:268
  26.2 13.8 %collective-permute-start.14 = (bf16[512,256]{1,0:T(8,128)(2,1)S(1)}, bf16[512,256]{1,0:T(8,128)(2,1)S(1)}, u32[]{:S(2)}, u32[]{:S(2)}) collective-permute-start(bf16[512,256]{1,0:T(8,128)(2,1)S(1)} %get-tuple-element.51), channel_id=1, source_target_pairs={{0,16},{8,24},{16,0},{24,8},{1,17},{9,25},{17,1},{25,9},{2,18},{10... | collective-permute-start | bytes 786440 | tf_op jit(solution)/shard_map/ppermute | solution.py:268
  27.8 12.8 %collective-permute-start.15 = (bf16[512,256]{1,0:T(8,128)(2,1)S(1)}, bf16[512,256]{1,0:T(8,128)(2,1)S(1)}, u32[]{:S(2)}, u32[]{:S(2)}) collective-permute-start(bf16[512,256]{1,0:T(8,128)(2,1)S(1)} %get-tuple-element.52), channel_id=1, source_target_pairs={{0,24},{8,16},{16,8},{24,0},{1,25},{9,17},{17,9},{25,1},{2,26},{10... | collective-permute-start | bytes 786440 | tf_op jit(solution)/shard_map/ppermute | solution.py:268
  31.7 20.7 %collective-permute-start.9 = (bf16[128,512]{1,0:T(8,128)(2,1)S(1)}, bf16[128,512]{1,0:T(8,128)(2,1)S(1)}, u32[]{:S(2)}, u32[]{:S(2)}) collective-permute-start(bf16[128,512]{1,0:T(8,128)(2,1)S(1)} %get-tuple-element.43), channel_id=1, source_target_pairs={{0,24},{8,0},{16,8},{24,16},{1,25},{9,1},{17,9},{25,17},{2,26},{10... | collective-permute-start | bytes 393224 | tf_op jit(solution)/shard_map/ppermute | solution.py:273
  34.0 18.4 %collective-permute-start.10 = (bf16[128,512]{1,0:T(8,128)(2,1)S(1)}, bf16[128,512]{1,0:T(8,128)(2,1)S(1)}, u32[]{:S(2)}, u32[]{:S(2)}) collective-permute-start(bf16[128,512]{1,0:T(8,128)(2,1)S(1)} %get-tuple-element.44), channel_id=1, source_target_pairs={{0,8},{8,16},{16,24},{24,0},{1,9},{9,17},{17,25},{25,1},{2,10},{10... | collective-permute-start | bytes 393224 | tf_op jit(solution)/shard_map/ppermute | solution.py:273
  40.7 7.6 %collective-permute-start.16 = (bf16[128,256]{1,0:T(8,128)(2,1)S(1)}, bf16[128,256]{1,0:T(8,128)(2,1)S(1)}, u32[]{:S(2)}, u32[]{:S(2)}) collective-permute-start(bf16[128,256]{1,0:T(8,128)(2,1)S(1)} %get-tuple-element.54), channel_id=1, source_target_pairs={{0,2},{1,3},{2,4},{3,5},{4,6},{5,7},{6,0},{7,1},{8,10},{9,11},{10,... | collective-permute-start | bytes 196616 | tf_op jit(solution)/shard_map/ppermute | solution.py:273
  42.5 7.4 %collective-permute-start.17 = (bf16[128,256]{1,0:T(8,128)(2,1)S(1)}, bf16[128,256]{1,0:T(8,128)(2,1)S(1)}, u32[]{:S(2)}, u32[]{:S(2)}) collective-permute-start(bf16[128,256]{1,0:T(8,128)(2,1)S(1)} %get-tuple-element.55), channel_id=1, source_target_pairs={{0,4},{1,5},{2,6},{3,7},{4,0},{5,1},{6,2},{7,3},{8,12},{9,13},{10,... | collective-permute-start | bytes 196616 | tf_op jit(solution)/shard_map/ppermute | solution.py:273
  45.7 4.6 %collective-permute-start.18 = (bf16[128,256]{1,0:T(8,128)(2,1)S(1)}, bf16[128,256]{1,0:T(8,128)(2,1)S(1)}, u32[]{:S(2)}, u32[]{:S(2)}) collective-permute-start(bf16[128,256]{1,0:T(8,128)(2,1)S(1)} %get-tuple-element.56), channel_id=1, source_target_pairs={{0,6},{1,7},{2,0},{3,1},{4,2},{5,3},{6,4},{7,5},{8,14},{9,15},{10,... | collective-permute-start | bytes 196616 | tf_op jit(solution)/shard_map/ppermute | solution.py:273
where the time goes:
time: 53.3 us; the launch traced here: 53 us
  starting transfers between devices  22.6 us (42%)
  waiting for transfers between devices  18.8 us (35%)
  Pallas kernels  10.2 us (19%)
  between operations  0.75 us (1%)
  local copies, waits for them, and re-layouts  0.67 us (1%)
    ppermute x12, waiting for transfers between devices, flip(): lax.ppermute(value, axis, [(i, i ^ mask) for i in range(lax.axis_size(axi...  15.5 us
    ppermute x7, starting transfers between devices, turn(): lax.ppermute(value, axis, [(i, (i + step) % count) for i in range(count)])  11.5 us
    ppermute x12, starting transfers between devices, flip(): lax.ppermute(value, axis, [(i, i ^ mask) for i in range(lax.axis_size(axi...  11.1 us
    pallas_call x11, Pallas kernels, call(): pl.pallas_call(body, out_shape=outs, in_specs=specs, out_specs=[vmem() fo...  10.2 us
    ppermute x7, waiting for transfers between devices, turn(): lax.ppermute(value, axis, [(i, (i + step) % count) for i in range(count)])  3.4 us
  transfers between devices with their start and end apart: 19, of which 8 were waited for; matrix products, arithmetic and copies ran while one was open for 0% of the time, Pallas kernels for 18%

commit v1 on v0

--- a/solution.py
+++ b/solution.py
@@ -157,7 +157,7 @@
     me = lax.axis_index("dp") // 2
     rows = outs[0].shape[0]
     for m, out in enumerate(outs):
-        at = pl.ds(pl.multiple_of(lax.rem(me + m, len(outs)) * rows, rows), rows)
+        at = pl.ds(pl.multiple_of((me ^ m) * rows, rows), rows)
         total = ins[0][at, :].astype(F32)
         for r in ins[1:]:
             total = total + r[at, :].astype(F32)
@@ -217,15 +217,24 @@
     half_ref[:, HEAD_WIDTH:] = part_v
 
 
-def backward_second_body(scale, place, q_ref, prev_ref, own_ref, next_ref, dy_ref, prob_ref, attf_ref, *rest):
-    pieces, whole_ref, half_ref = rest[:2], rest[2], rest[3]
-    outs, ds_ref = rest[4:7], rest[7]
+def backward_second_body(place, q_ref, prev_ref, own_ref, next_ref, dy_ref, prob_ref, attf_ref, *rest):
+    piece, half_ref, more_ref, ds_ref = rest
+    head, group = place()
+    shared = (q_ref, (prev_ref, own_ref, next_ref), dy_ref, prob_ref, attf_ref)
+    part_k, part_v = heads_backward([head(6)], group(6), *shared, [piece], ds_ref, 0)
+    more_ref[:, :HEAD_WIDTH] = part_k + half_ref[:, :HEAD_WIDTH]
+    more_ref[:, HEAD_WIDTH:] = part_v + half_ref[:, HEAD_WIDTH:]
+
+
+def backward_third_body(scale, place, q_ref, prev_ref, own_ref, next_ref, dy_ref, prob_ref, attf_ref, *rest):
+    piece, whole_ref, half_ref = rest[:3]
+    outs, ds_ref = rest[3:6], rest[6]
     head, group = place()
     tokens = q_ref.shape[0]
     width = own_ref.shape[1] // 2
     band = (prev_ref, own_ref, next_ref)
     shared = (q_ref, band, dy_ref, prob_ref, attf_ref)
-    part_k, part_v = heads_backward([head(j) for j in (6, 7)], group(6), *shared, pieces, ds_ref, 0)
+    part_k, part_v = heads_backward([head(7)], group(6), *shared, [piece], ds_ref, 0)
     part_k = ((part_k + half_ref[:, :HEAD_WIDTH]) * scale).astype(BF16)
     part_v = (part_v + half_ref[:, HEAD_WIDTH:]).astype(BF16)
     for t, out in enumerate(outs):
@@ -236,11 +245,11 @@
         out[:, lanes_at(width + group(0) * HEAD_WIDTH)] = whole_ref[rows, HEAD_WIDTH:]
 
 
-def output_body(scale, place, prev_ref, own_ref, next_ref, ds_ref, ds_last_ref, att_ref, *rest):
+def output_body(scale, place, prev_ref, own_ref, next_ref, ds_ref, ds_more_ref, ds_last_ref, att_ref, *rest):
     pieces, (mixed_ref, gq_ref) = rest[:QUERY_HEADS], rest[QUERY_HEADS:]
     head, group = place()
     tokens = mixed_ref.shape[0]
-    ds = (ds_ref[:, : 4 * HEAD_WIDTH], jnp.concatenate([ds_ref[:, 4 * HEAD_WIDTH :], ds_last_ref[...]], 1))
+    ds = (ds_ref[:, : 4 * HEAD_WIDTH], jnp.concatenate([ds_ref[:, 4 * HEAD_WIDTH :], ds_more_ref[...], ds_last_ref[...]], 1))
     for half in range(2):
         keys = band_of((prev_ref, own_ref, next_ref), tokens, group(4 * half) * HEAD_WIDTH)
         dq = dot(keys.T, ds[half], NN) * scale
@@ -354,7 +363,7 @@
         )
         landed = [blocks[0]]
         for m in range(1, n_z):
-            landed.append(turn(blocks[m], "dp", 2 * m))
+            landed.append(flip(blocks[m], "dp", 2 * m))
         grad_weight = call(
             functools.partial(weight_sum_body, norm_factor),
             [shape((half // n_z, column_width), F32)],
@@ -378,20 +387,29 @@
         (q, prev_kv, own, next_kv, dy, prob, attf, *pieces[:6]),
         flops=(2 * macs * model + 6 * macs * band) * 3 // 4,
     )
+    shared = (q, prev_kv, own, next_kv, dy, prob, attf)
+    one_head = (2 * macs * model + 6 * macs * band) // QUERY_HEADS
+    half_sum, ds_more = call(
+        functools.partial(backward_second_body, place),
+        [shape((band, 2 * HEAD_WIDTH), F32), shape((band, HEAD_WIDTH))],
+        [vmem()] * 9,
+        (*shared, pieces[6], half_sum),
+        flops=one_head,
+    )
     low, mid, high, ds_last = call(
-        functools.partial(backward_second_body, scale, place),
-        [shape((tokens, 2 * kv_width))] * 3 + [shape((band, 2 * HEAD_WIDTH))],
-        [vmem()] * 11,
-        (q, prev_kv, own, next_kv, dy, prob, attf, *pieces[6:], whole, half_sum),
-        flops=(2 * macs * model + 6 * macs * band) // 4,
+        functools.partial(backward_third_body, scale, place),
+        [shape((tokens, 2 * kv_width))] * 3 + [shape((band, HEAD_WIDTH))],
+        [vmem()] * 10,
+        (*shared, pieces[7], whole, half_sum),
+        flops=one_head,
     )
     from_next = turn(low, "ctx", -1)
     from_prev = turn(high, "ctx", 1)
     mixed, grad_q = call(
         functools.partial(output_body, scale, place),
         [shape((tokens, model)), shape((tokens, query_width))],
-        [vmem()] * 14,
-        (prev_kv, own, next_kv, ds, ds_last, att, *pieces),
+        [vmem()] * 15,
+        (prev_kv, own, next_kv, ds, ds_more, ds_last, att, *pieces),
         flops=2 * macs * model + 2 * macs * band,
     )
     grad_k, grad_v = call(key_value_body, [shape((tokens, kv_width))] * 2, [vmem()] * 3, (mid, from_next, from_prev))

time: 53.3 us -> 54.8 us (1.028)
  waiting for transfers between devices: 18.8 us -> 21.2 us
  starting transfers between devices: 22.6 us -> 21.4 us
    ppermute x7 -> x4, starting transfers between devices: 11.5 us -> 5.27 us  [turn(): lax.ppermute(value, axis, [(i, (i + step) % count) for i in range(count)])]
    ppermute x12 -> x15, waiting for transfers between devices: 15.5 us -> 21.2 us  [flip(): lax.ppermute(value, axis, [(i, i ^ mask) for i in range(lax.axis_size(axi...]
    ppermute x12 -> x15, starting transfers between devices: 11.1 us -> 16.2 us  [flip(): lax.ppermute(value, axis, [(i, i ^ mask) for i in range(lax.axis_size(axi...]
    ppermute x7 -> x4, waiting for transfers between devices: 3.4 us -> 0.01 us  [turn(): lax.ppermute(value, axis, [(i, (i + step) % count) for i in range(count)])]
    pallas_call x11 -> x12, Pallas kernels: 10.2 us -> 10.5 us  [call(): pl.pallas_call(body, out_shape=outs, in_specs=specs, out_specs=[vmem() fo...]
  transfers between devices with their start and end apart: 19 -> 19, of which waited for: 8 -> 6; matrix products, arithmetic and copies ran while one was open for 0% -> 0% of each run, Pallas kernels for 18% -> 18%
where the time goes in v1:
time: 54.8 us; the launch traced here: 54.6 us
  starting transfers between devices  21.4 us (39%)
  waiting for transfers between devices  21.2 us (39%)
  Pallas kernels  10.5 us (19%)
  between operations  0.76 us (1%)
  local copies, waits for them, and re-layouts  0.67 us (1%)
    ppermute x15, waiting for transfers between devices, flip(): lax.ppermute(value, axis, [(i, i ^ mask) for i in range(lax.axis_size(axi...  21.2 us
    ppermute x15, starting transfers between devices, flip(): lax.ppermute(value, axis, [(i, i ^ mask) for i in range(lax.axis_size(axi...  16.2 us
    pallas_call x12, Pallas kernels, call(): pl.pallas_call(body, out_shape=outs, in_specs=specs, out_specs=[vmem() fo...  10.5 us
    ppermute x4, starting transfers between devices, turn(): lax.ppermute(value, axis, [(i, (i + step) % count) for i in range(count)])  5.27 us
  transfers between devices with their start and end apart: 19, of which 6 were waited for; matrix products, arithmetic and copies ran while one was open for 0% of the time, Pallas kernels for 18%

profile of v1, /device:TPU:0, one launch (start us, length us, event | category | flops | bytes accessed | tf_op | source)
XLA Modules:
  0.0 54.6 jit_solution(1541636007624704712)
XLA Ops:
  0.6 0.0 copy-start
  0.6 4.1 %collective-permute-start.5 = (bf16[128,1024]{1,0:T(8,128)(2,1)}, bf16[128,1024]{1,0:T(8,128)(2,1)S(1)}, u32[]{:S(2)}, u32[]{:S(2)}) collective-permute-start(bf16[128,1024]{1,0:T(8,128)(2,1)} %rest_0_.3), channel_id=1, source_target_pairs={{0,4},{1,5},{2,6},{3,7},{4,0},{5,1},{6,2},{7,3},{8,12},{9,13},{10,... | collective-permute-start | bytes 786440 | tf_op jit(solution)/shard_map/ppermute | solution.py:277
  4.8 1.6 %collective-permute-start.3 = (bf16[128,1024]{1,0:T(8,128)(2,1)}, bf16[128,1024]{1,0:T(8,128)(2,1)S(1)}, u32[]{:S(2)}, u32[]{:S(2)}) collective-permute-start(bf16[128,1024]{1,0:T(8,128)(2,1)} %rest_0_.3), channel_id=1, source_target_pairs={{0,2},{1,3},{2,0},{3,1},{4,6},{5,7},{6,4},{7,5},{8,10},{9,11},{10,... | collective-permute-start | bytes 786440 | tf_op jit(solution)/shard_map/ppermute | solution.py:277
  6.3 0.9 %shard_map.110.own_ref = bf16[136,512]{1,0:T(8,128)(2,1)S(1)} custom-call(bf16[128,256]{1,0:T(8,128)(2,1)} %bitcast.14, bf16[128,256]{1,0:T(8,128)(2,1)} %bitcast.15, s32[1,128]{1,0:T(1,128)} %bitcast.16), custom_call_target="tpu_custom_call" | custom-call | flops 1048576 | bytes 270848 | tf_op jit(solution)/shard_map/pallas_call | solution.py:47
  7.3 1.5 %collective-permute-start = (bf16[136,512]{1,0:T(8,128)(2,1)S(1)}, bf16[136,512]{1,0:T(8,128)(2,1)S(1)}, u32[]{:S(2)}, u32[]{:S(2)}) collective-permute-start(bf16[136,512]{1,0:T(8,128)(2,1)S(1)} %shard_map.110.own_ref), channel_id=1, source_target_pairs={{0,8},{8,16},{16,24},{24,0},{1,9},{9,17},{17,25},{25,1},{2,10},{10... | collective-permute-start | bytes 417800 | tf_op jit(solution)/shard_map/ppermute | solution.py:282
  8.8 0.0 collective-permute-start.12
  8.8 1.4 %collective-permute-start.1 = (bf16[136,512]{1,0:T(8,128)(2,1)S(1)}, bf16[136,512]{1,0:T(8,128)(2,1)S(1)}, u32[]{:S(2)}, u32[]{:S(2)}) collective-permute-start(bf16[136,512]{1,0:T(8,128)(2,1)S(1)} %shard_map.110.own_ref), channel_id=1, source_target_pairs={{0,24},{8,0},{16,8},{24,16},{1,25},{9,1},{17,9},{25,17},{2,26},{10... | collective-permute-start | bytes 417800 | tf_op jit(solution)/shard_map/ppermute | solution.py:282
  10.2 6.8 %collective-permute-done.5.rest_4_ = bf16[128,1024]{1,0:T(8,128)(2,1)S(1)} collective-permute-done((bf16[128,1024]{1,0:T(8,128)(2,1)}, bf16[128,1024]{1,0:T(8,128)(2,1)S(1)}, u32[]{:S(2)}, u32[]{:S(2)}) %collective-permute-start.5) | collective-permute-done | bytes 262176 | tf_op jit(solution)/shard_map/ppermute | solution.py:277
  17.0 0.7 %collective-permute-start.7 = (bf16[128,1024]{1,0:T(8,128)(2,1)S(1)}, bf16[128,1024]{1,0:T(8,128)(2,1)S(1)}, u32[]{:S(2)}, u32[]{:S(2)}) collective-permute-start(bf16[128,1024]{1,0:T(8,128)(2,1)S(1)} %collective-permute-done.5.rest_4_), channel_id=1, source_target_pairs={{0,2},{1,3},{2,0},{3,1},{4,6},{5,7},{6,4},{7,5},{8,10},{9,11},{10,... | collective-permute-start | bytes 786440 | tf_op jit(solution)/shard_map/ppermute | solution.py:277
  17.7 0.0 collective-permute-done.prev_ref
  17.7 0.0 copy-done
  17.7 0.0 collective-permute-start.2
  17.7 0.0 collective-permute-done.3.rest_2_
  17.8 0.5 collective-permute-start.4
  18.3 1.0 %shard_map.111 = (bf16[128,1024]{1,0:T(8,128)(2,1)S(1)}, bf16[128,1024]{1,0:T(8,128)(2,1)S(1)}) custom-call(bf16[128,1024]{1,0:T(8,128)(2,1)} %bitcast.11, bf16[128,1024]{1,0:T(8,128)(2,1)} %bitcast.13), custom_call_target="tpu_custom_call" | custom-call | flops 1048576 | bytes 1048576 | tf_op jit(solution)/shard_map/pallas_call | solution.py:47
  19.3 0.0 copy-start.1
  19.3 0.0 collective-permute-done.1.next_ref
  19.3 0.7 %copy-done.1 = s32[1,4,8]{2,1,0:T(4,128)S(1)} copy-done((s32[1,4,8]{2,1,0:T(4,128)S(1)}, s32[1,4,8]{2,1,0:T(4,128)}, u32[]{:S(2)}) %copy-start.1) | copy-done | bytes 152
  20.0 1.7 %shard_map.112 = (bf16[384,1024]{1,0:T(8,128)(2,1)S(1)}, f32[1024,128]{1,0:T(8,128)S(1)}, bf16[1024,128]{1,0:T(8,128)(2,1)S(1)}) custom-call(bf16[128,1024]{1,0:T(8,128)(2,1)S(1)} %get-tuple-element.33.q_ref, bf16[136,512]{1,0:T(8,128)(2,1)S(1)} %collective-permute-done.prev_ref, bf16[136,512]{1,0:T(8,128)(2,1)S(1)} %shard_map.110.own_ref, ...), custom_call_target="tpu_custom_call" | custom-call | flops 201326592 | bytes 2252928 | tf_op jit(solution)/shard_map/pallas_call | solution.py:47
  21.7 0.1 collective-permute-start.11
  21.9 0.0 collective-permute-done.12.dy_other_ref
  21.9 0.4 collective-permute-start.6
  22.3 2.1 %collective-permute-done.7.rest_0_.rest_6_ = bf16[128,1024]{1,0:T(8,128)(2,1)S(1)} collective-permute-done((bf16[128,1024]{1,0:T(8,128)(2,1)S(1)}, bf16[128,1024]{1,0:T(8,128)(2,1)S(1)}, u32[]{:S(2)}, u32[]{:S(2)}) %collective-permute-start.7) | collective-permute-done | bytes 262176 | tf_op jit(solution)/shard_map/ppermute | solution.py:277
  24.4 0.0 collective-permute-start.8
  24.4 0.0 collective-permute-done.11.other_ref
  24.4 0.5 shard_map.119
  24.9 1.4 %collective-permute-start.13 = (bf16[512,256]{1,0:T(8,128)(2,1)S(1)}, bf16[512,256]{1,0:T(8,128)(2,1)S(1)}, u32[]{:S(2)}, u32[]{:S(2)}) collective-permute-start(bf16[512,256]{1,0:T(8,128)(2,1)S(1)} %get-tuple-element.54), channel_id=1, source_target_pairs={{0,8},{8,0},{16,24},{24,16},{1,9},{9,1},{17,25},{25,17},{2,10},{10... | collective-permute-start | bytes 786440 | tf_op jit(solution)/shard_map/ppermute | solution.py:277
  26.2 0.0 collective-permute-done.2.rest_1_
  26.2 1.5 %collective-permute-start.14 = (bf16[512,256]{1,0:T(8,128)(2,1)S(1)}, bf16[512,256]{1,0:T(8,128)(2,1)S(1)}, u32[]{:S(2)}, u32[]{:S(2)}) collective-permute-start(bf16[512,256]{1,0:T(8,128)(2,1)S(1)} %get-tuple-element.55), channel_id=1, source_target_pairs={{0,16},{8,24},{16,0},{24,8},{1,17},{9,25},{17,1},{25,9},{2,18},{10... | collective-permute-start | bytes 786440 | tf_op jit(solution)/shard_map/ppermute | solution.py:277
  27.8 0.0 collective-permute-done.4.rest_3_
  27.8 0.7 %collective-permute-start.15 = (bf16[512,256]{1,0:T(8,128)(2,1)S(1)}, bf16[512,256]{1,0:T(8,128)(2,1)S(1)}, u32[]{:S(2)}, u32[]{:S(2)}) collective-permute-start(bf16[512,256]{1,0:T(8,128)(2,1)S(1)} %get-tuple-element.56), channel_id=1, source_target_pairs={{0,24},{8,16},{16,8},{24,0},{1,25},{9,17},{17,9},{25,1},{2,26},{10... | collective-permute-start | bytes 786440 | tf_op jit(solution)/shard_map/ppermute | solution.py:277
  28.5 0.0 collective-permute-done.6.rest_5_
  28.5 2.2 %shard_map.113 = (bf16[384,256]{1,0:T(8,128)(2,1)S(1)}, f32[384,256]{1,0:T(8,128)S(1)}, bf16[384,768]{1,0:T(8,128)(2,1)S(1)}) custom-call(bf16[128,1024]{1,0:T(8,128)(2,1)S(1)} %get-tuple-element.33.q_ref, bf16[136,512]{1,0:T(8,128)(2,1)S(1)} %collective-permute-done.prev_ref, bf16[136,512]{1,0:T(8,128)(2,1)S(1)} %shard_map.110.own_ref, ...), custom_call_target="tpu_custom_call" | custom-call | flops 427819008 | bytes 5005312 | tf_op jit(solution)/shard_map/pallas_call | solution.py:47
  30.7 0.6 %shard_map.114 = (f32[384,256]{1,0:T(8,128)S(1)}, bf16[384,128]{1,0:T(8,128)(2,1)S(1)}) custom-call(bf16[128,1024]{1,0:T(8,128)(2,1)S(1)} %get-tuple-element.33.q_ref, bf16[136,512]{1,0:T(8,128)(2,1)S(1)} %collective-permute-done.prev_ref, bf16[136,512]{1,0:T(8,128)(2,1)S(1)} %shard_map.110.own_ref, bf16[136,512]{1,0:T(8,128)(2,1)S(1)} %collective-permute-done.1.next_ref, ...), custom_call_target="tpu_custom_call" | custom-call | flops 71303168 | bytes 3399680 | tf_op jit(solution)/shard_map/pallas_call | solution.py:47
  31.3 0.0 collective-permute-done.8.rest_0_.rest_7_
  31.3 0.7 %shard_map.115 = (bf16[128,512]{1,0:T(8,128)(2,1)S(1)}, bf16[128,512]{1,0:T(8,128)(2,1)S(1)}, bf16[128,512]{1,0:T(8,128)(2,1)S(1)}, bf16[384,128]{1,0:T(8,128)(2,1)S(1)}) custom-call(bf16[128,1024]{1,0:T(8,128)(2,1)S(1)} %get-tuple-element.33.q_ref, bf16[136,512]{1,0:T(8,128)(2,1)S(1)} %collective-permute-done.prev_ref, ...), custom_call_target="tpu_custom_call" | custom-call | flops 71303168 | bytes 3596288 | tf_op jit(solution)/shard_map/pallas_call | solution.py:47
  32.0 2.3 %collective-permute-start.9 = (bf16[128,512]{1,0:T(8,128)(2,1)S(1)}, bf16[128,512]{1,0:T(8,128)(2,1)S(1)}, u32[]{:S(2)}, u32[]{:S(2)}) collective-permute-start(bf16[128,512]{1,0:T(8,128)(2,1)S(1)} %get-tuple-element.47), channel_id=1, source_target_pairs={{0,24},{8,0},{16,8},{24,16},{1,25},{9,1},{17,9},{25,17},{2,26},{10... | collective-permute-start | bytes 393224 | tf_op jit(solution)/shard_map/ppermute | solution.py:282
  34.3 0.0 collective-permute-start.10
  34.3 0.0 collective-permute-done.13.refs_1_
  34.3 5.8 %collective-permute-done.14.refs_2_ = bf16[512,256]{1,0:T(8,128)(2,1)S(1)} collective-permute-done((bf16[512,256]{1,0:T(8,128)(2,1)S(1)}, bf16[512,256]{1,0:T(8,128)(2,1)S(1)}, u32[]{:S(2)}, u32[]{:S(2)}) %collective-permute-start.14) | collective-permute-done | bytes 262176 | tf_op jit(solution)/shard_map/ppermute | solution.py:277
  40.1 0.5 collective-permute-done.15.refs_3_
  40.5 0.1 shard_map.120
  40.7 1.8 %collective-permute-start.16 = (bf16[128,256]{1,0:T(8,128)(2,1)S(1)}, bf16[128,256]{1,0:T(8,128)(2,1)S(1)}, u32[]{:S(2)}, u32[]{:S(2)}) collective-permute-start(bf16[128,256]{1,0:T(8,128)(2,1)S(1)} %get-tuple-element.58), channel_id=1, source_target_pairs={{0,2},{1,3},{2,0},{3,1},{4,6},{5,7},{6,4},{7,5},{8,10},{9,11},{10,... | collective-permute-start | bytes 196616 | tf_op jit(solution)/shard_map/ppermute | solution.py:277
  42.5 3.3 %collective-permute-start.17 = (bf16[128,256]{1,0:T(8,128)(2,1)S(1)}, bf16[128,256]{1,0:T(8,128)(2,1)S(1)}, u32[]{:S(2)}, u32[]{:S(2)}) collective-permute-start(bf16[128,256]{1,0:T(8,128)(2,1)S(1)} %get-tuple-element.59), channel_id=1, source_target_pairs={{0,4},{1,5},{2,6},{3,7},{4,0},{5,1},{6,2},{7,3},{8,12},{9,13},{10,... | collective-permute-start | bytes 196616 | tf_op jit(solution)/shard_map/ppermute | solution.py:277
  45.8 0.0 collective-permute-start.18
  45.8 0.0 collective-permute-done.16.refs_1_
  45.8 4.0 %collective-permute-done.17.refs_2_ = bf16[128,256]{1,0:T(8,128)(2,1)S(1)} collective-permute-done((bf16[128,256]{1,0:T(8,128)(2,1)S(1)}, bf16[128,256]{1,0:T(8,128)(2,1)S(1)}, u32[]{:S(2)}, u32[]{:S(2)}) %collective-permute-start.17) | collective-permute-done | bytes 65568 | tf_op jit(solution)/shard_map/ppermute | solution.py:277
  49.7 2.1 %collective-permute-done.18.refs_3_ = bf16[128,256]{1,0:T(8,128)(2,1)S(1)} collective-permute-done((bf16[128,256]{1,0:T(8,128)(2,1)S(1)}, bf16[128,256]{1,0:T(8,128)(2,1)S(1)}, u32[]{:S(2)}, u32[]{:S(2)}) %collective-permute-start.18) | collective-permute-done | bytes 65568 | tf_op jit(solution)/shard_map/ppermute | solution.py:277
  51.8 0.7 %shard_map.121 = f32[128,256]{1,0:T(8,128)} custom-call(bf16[128,256]{1,0:T(8,128)(2,1)S(1)} %get-tuple-element.57.refs_0_, bf16[128,256]{1,0:T(8,128)(2,1)S(1)} %collective-permute-done.16.refs_1_, bf16[128,256]{1,0:T(8,128)(2,1)S(1)} %collective-permute-done.17.refs_2_, bf16[128,256]{1,0:T(8,128)(2,1)S(1)} %collective-permute-done.18.refs_3_), custom_call_target="tpu_custom_call" | custom-call | flops 1048576 | bytes 393216 | tf_op jit(solution)/shard_map/pallas_call | solution.py:47
  52.5 1.4 %shard_map.116 = (bf16[128,1024]{1,0:T(8,128)(2,1)}, bf16[128,1024]{1,0:T(8,128)(2,1)}) custom-call(bf16[136,512]{1,0:T(8,128)(2,1)S(1)} %collective-permute-done.prev_ref, bf16[136,512]{1,0:T(8,128)(2,1)S(1)} %shard_map.110.own_ref, bf16[136,512]{1,0:T(8,128)(2,1)S(1)} %collective-permute-done.1.next_ref, bf16[384,768]{1,0:T(8,128)(2,1)S(1)} %get-tuple-element.37.ds_ref, ...), custom_call_target="tpu_custom_call" | custom-call | flops 369098752 | bytes 4087808 | tf_op jit(solution)/shard_map/pallas_call | solution.py:47
  53.9 0.0 collective-permute-done.9.low_ref
  53.9 0.0 collective-permute-done.10.high_ref
  53.9 0.7 %shard_map.117 = (bf16[128,256]{1,0:T(8,128)(2,1)}, bf16[128,256]{1,0:T(8,128)(2,1)}) custom-call(bf16[128,512]{1,0:T(8,128)(2,1)S(1)} %get-tuple-element.46.own_ref, bf16[128,512]{1,0:T(8,128)(2,1)S(1)} %collective-permute-done.9.low_ref, bf16[128,512]{1,0:T(8,128)(2,1)S(1)} %collective-permute-done.10.high_ref), custom_call_target="tpu_custom_call" | custom-call | flops 1048576 | bytes 524288 | tf_op jit(solution)/shard_map/pallas_call | solution.py:47
  (1 shorter events, 0.0 us)
Async XLA Ops:
  0.6 17.1 %copy-start = (bf16[128,1024]{1,0:T(8,128)(2,1)S(1)}, bf16[128,1024]{1,0:T(8,128)(2,1)}, u32[]{:S(2)}) copy-start(bf16[128,1024]{1,0:T(8,128)(2,1)} %rest_0_.3) | copy-start | bytes 786436
  0.6 16.4 %collective-permute-start.5 = (bf16[128,1024]{1,0:T(8,128)(2,1)}, bf16[128,1024]{1,0:T(8,128)(2,1)S(1)}, u32[]{:S(2)}, u32[]{:S(2)}) collective-permute-start(bf16[128,1024]{1,0:T(8,128)(2,1)} %rest_0_.3), channel_id=1, source_target_pairs={{0,4},{1,5},{2,6},{3,7},{4,0},{5,1},{6,2},{7,3},{8,12},{9,13},{10,... | collective-permute-start | bytes 786440 | tf_op jit(solution)/shard_map/ppermute | solution.py:277
  4.8 13.0 %collective-permute-start.3 = (bf16[128,1024]{1,0:T(8,128)(2,1)}, bf16[128,1024]{1,0:T(8,128)(2,1)S(1)}, u32[]{:S(2)}, u32[]{:S(2)}) collective-permute-start(bf16[128,1024]{1,0:T(8,128)(2,1)} %rest_0_.3), channel_id=1, source_target_pairs={{0,2},{1,3},{2,0},{3,1},{4,6},{5,7},{6,4},{7,5},{8,10},{9,11},{10,... | collective-permute-start | bytes 786440 | tf_op jit(solution)/shard_map/ppermute | solution.py:277
  7.3 10.5 %collective-permute-start = (bf16[136,512]{1,0:T(8,128)(2,1)S(1)}, bf16[136,512]{1,0:T(8,128)(2,1)S(1)}, u32[]{:S(2)}, u32[]{:S(2)}) collective-permute-start(bf16[136,512]{1,0:T(8,128)(2,1)S(1)} %shard_map.110.own_ref), channel_id=1, source_target_pairs={{0,8},{8,16},{16,24},{24,0},{1,9},{9,17},{17,25},{25,1},{2,10},{10... | collective-permute-start | bytes 417800 | tf_op jit(solution)/shard_map/ppermute | solution.py:282
  8.8 13.1 %collective-permute-start.12 = (bf16[128,1024]{1,0:T(8,128)(2,1)}, bf16[128,1024]{1,0:T(8,128)(2,1)S(1)}, u32[]{:S(2)}, u32[]{:S(2)}) collective-permute-start(bf16[128,1024]{1,0:T(8,128)(2,1)} %bitcast.12), channel_id=1, source_target_pairs={{0,1},{1,0},{2,3},{3,2},{4,5},{5,4},{6,7},{7,6},{8,9},{9,8},{10,11... | collective-permute-start | bytes 786440 | tf_op jit(solution)/shard_map/ppermute | solution.py:277
  8.8 10.5 %collective-permute-start.1 = (bf16[136,512]{1,0:T(8,128)(2,1)S(1)}, bf16[136,512]{1,0:T(8,128)(2,1)S(1)}, u32[]{:S(2)}, u32[]{:S(2)}) collective-permute-start(bf16[136,512]{1,0:T(8,128)(2,1)S(1)} %shard_map.110.own_ref), channel_id=1, source_target_pairs={{0,24},{8,0},{16,8},{24,16},{1,25},{9,1},{17,9},{25,17},{2,26},{10... | collective-permute-start | bytes 417800 | tf_op jit(solution)/shard_map/ppermute | solution.py:282
  17.0 7.4 %collective-permute-start.7 = (bf16[128,1024]{1,0:T(8,128)(2,1)S(1)}, bf16[128,1024]{1,0:T(8,128)(2,1)S(1)}, u32[]{:S(2)}, u32[]{:S(2)}) collective-permute-start(bf16[128,1024]{1,0:T(8,128)(2,1)S(1)} %collective-permute-done.5.rest_4_), channel_id=1, source_target_pairs={{0,2},{1,3},{2,0},{3,1},{4,6},{5,7},{6,4},{7,5},{8,10},{9,11},{10,... | collective-permute-start | bytes 786440 | tf_op jit(solution)/shard_map/ppermute | solution.py:277
  17.7 8.5 %collective-permute-start.2 = (bf16[128,1024]{1,0:T(8,128)(2,1)S(1)}, bf16[128,1024]{1,0:T(8,128)(2,1)S(1)}, u32[]{:S(2)}, u32[]{:S(2)}) collective-permute-start(bf16[128,1024]{1,0:T(8,128)(2,1)S(1)} %copy-done), channel_id=1, source_target_pairs={{0,1},{1,0},{2,3},{3,2},{4,5},{5,4},{6,7},{7,6},{8,9},{9,8},{10,11... | collective-permute-start | bytes 786440 | tf_op jit(solution)/shard_map/ppermute | solution.py:277
  17.8 10.0 %collective-permute-start.4 = (bf16[128,1024]{1,0:T(8,128)(2,1)S(1)}, bf16[128,1024]{1,0:T(8,128)(2,1)S(1)}, u32[]{:S(2)}, u32[]{:S(2)}) collective-permute-start(bf16[128,1024]{1,0:T(8,128)(2,1)S(1)} %collective-permute-done.3.rest_2_), channel_id=1, source_target_pairs={{0,1},{1,0},{2,3},{3,2},{4,5},{5,4},{6,7},{7,6},{8,9},{9,8},{10,11... | collective-permute-start | bytes 786440 | tf_op jit(solution)/shard_map/ppermute | solution.py:277
  19.3 0.7 %copy-start.1 = (s32[1,4,8]{2,1,0:T(4,128)S(1)}, s32[1,4,8]{2,1,0:T(4,128)}, u32[]{:S(2)}) copy-start(s32[1,4,8]{2,1,0:T(4,128)} %param.11) | copy-start | bytes 388
  21.7 2.7 %collective-permute-start.11 = (bf16[512,128]{1,0:T(8,128)(2,1)S(1)}, bf16[512,128]{1,0:T(8,128)(2,1)S(1)}, u32[]{:S(2)}, u32[]{:S(2)}) collective-permute-start(bf16[512,128]{1,0:T(8,128)(2,1)S(1)} %get-tuple-element.52), channel_id=1, source_target_pairs={{0,1},{1,0},{2,3},{3,2},{4,5},{5,4},{6,7},{7,6},{8,9},{9,8},{10,11... | collective-permute-start | bytes 393224 | tf_op jit(solution)/shard_map/ppermute | solution.py:277
  21.9 6.6 %collective-permute-start.6 = (bf16[128,1024]{1,0:T(8,128)(2,1)S(1)}, bf16[128,1024]{1,0:T(8,128)(2,1)S(1)}, u32[]{:S(2)}, u32[]{:S(2)}) collective-permute-start(bf16[128,1024]{1,0:T(8,128)(2,1)S(1)} %collective-permute-done.5.rest_4_), channel_id=1, source_target_pairs={{0,1},{1,0},{2,3},{3,2},{4,5},{5,4},{6,7},{7,6},{8,9},{9,8},{10,11... | collective-permute-start | bytes 786440 | tf_op jit(solution)/shard_map/ppermute | solution.py:277
  24.4 6.9 %collective-permute-start.8 = (bf16[128,1024]{1,0:T(8,128)(2,1)S(1)}, bf16[128,1024]{1,0:T(8,128)(2,1)S(1)}, u32[]{:S(2)}, u32[]{:S(2)}) collective-permute-start(bf16[128,1024]{1,0:T(8,128)(2,1)S(1)} %collective-permute-done.7.rest_0_.rest_6_), channel_id=1, source_target_pairs={{0,1},{1,0},{2,3},{3,2},{4,5},{5,4},{6,7},{7,6},{8,9},{9,8},{10,11... | collective-permute-start | bytes 786440 | tf_op jit(solution)/shard_map/ppermute | solution.py:277
  24.9 9.4 %collective-permute-start.13 = (bf16[512,256]{1,0:T(8,128)(2,1)S(1)}, bf16[512,256]{1,0:T(8,128)(2,1)S(1)}, u32[]{:S(2)}, u32[]{:S(2)}) collective-permute-start(bf16[512,256]{1,0:T(8,128)(2,1)S(1)} %get-tuple-element.54), channel_id=1, source_target_pairs={{0,8},{8,0},{16,24},{24,16},{1,9},{9,1},{17,25},{25,17},{2,10},{10... | collective-permute-start | bytes 786440 | tf_op jit(solution)/shard_map/ppermute | solution.py:277
  26.2 13.8 %collective-permute-start.14 = (bf16[512,256]{1,0:T(8,128)(2,1)S(1)}, bf16[512,256]{1,0:T(8,128)(2,1)S(1)}, u32[]{:S(2)}, u32[]{:S(2)}) collective-permute-start(bf16[512,256]{1,0:T(8,128)(2,1)S(1)} %get-tuple-element.55), channel_id=1, source_target_pairs={{0,16},{8,24},{16,0},{24,8},{1,17},{9,25},{17,1},{25,9},{2,18},{10... | collective-permute-start | bytes 786440 | tf_op jit(solution)/shard_map/ppermute | solution.py:277
  27.8 12.8 %collective-permute-start.15 = (bf16[512,256]{1,0:T(8,128)(2,1)S(1)}, bf16[512,256]{1,0:T(8,128)(2,1)S(1)}, u32[]{:S(2)}, u32[]{:S(2)}) collective-permute-start(bf16[512,256]{1,0:T(8,128)(2,1)S(1)} %get-tuple-element.56), channel_id=1, source_target_pairs={{0,24},{8,16},{16,8},{24,0},{1,25},{9,17},{17,9},{25,1},{2,26},{10... | collective-permute-start | bytes 786440 | tf_op jit(solution)/shard_map/ppermute | solution.py:277
  32.0 21.9 %collective-permute-start.9 = (bf16[128,512]{1,0:T(8,128)(2,1)S(1)}, bf16[128,512]{1,0:T(8,128)(2,1)S(1)}, u32[]{:S(2)}, u32[]{:S(2)}) collective-permute-start(bf16[128,512]{1,0:T(8,128)(2,1)S(1)} %get-tuple-element.47), channel_id=1, source_target_pairs={{0,24},{8,0},{16,8},{24,16},{1,25},{9,1},{17,9},{25,17},{2,26},{10... | collective-permute-start | bytes 393224 | tf_op jit(solution)/shard_map/ppermute | solution.py:282
  34.3 19.6 %collective-permute-start.10 = (bf16[128,512]{1,0:T(8,128)(2,1)S(1)}, bf16[128,512]{1,0:T(8,128)(2,1)S(1)}, u32[]{:S(2)}, u32[]{:S(2)}) collective-permute-start(bf16[128,512]{1,0:T(8,128)(2,1)S(1)} %get-tuple-element.48), channel_id=1, source_target_pairs={{0,8},{8,16},{16,24},{24,0},{1,9},{9,17},{17,25},{25,1},{2,10},{10... | collective-permute-start | bytes 393224 | tf_op jit(solution)/shard_map/ppermute | solution.py:282
  40.7 5.1 %collective-permute-start.16 = (bf16[128,256]{1,0:T(8,128)(2,1)S(1)}, bf16[128,256]{1,0:T(8,128)(2,1)S(1)}, u32[]{:S(2)}, u32[]{:S(2)}) collective-permute-start(bf16[128,256]{1,0:T(8,128)(2,1)S(1)} %get-tuple-element.58), channel_id=1, source_target_pairs={{0,2},{1,3},{2,0},{3,1},{4,6},{5,7},{6,4},{7,5},{8,10},{9,11},{10,... | collective-permute-start | bytes 196616 | tf_op jit(solution)/shard_map/ppermute | solution.py:277
  42.5 7.2 %collective-permute-start.17 = (bf16[128,256]{1,0:T(8,128)(2,1)S(1)}, bf16[128,256]{1,0:T(8,128)(2,1)S(1)}, u32[]{:S(2)}, u32[]{:S(2)}) collective-permute-start(bf16[128,256]{1,0:T(8,128)(2,1)S(1)} %get-tuple-element.59), channel_id=1, source_target_pairs={{0,4},{1,5},{2,6},{3,7},{4,0},{5,1},{6,2},{7,3},{8,12},{9,13},{10,... | collective-permute-start | bytes 196616 | tf_op jit(solution)/shard_map/ppermute | solution.py:277
  45.8 6.1 %collective-permute-start.18 = (bf16[128,256]{1,0:T(8,128)(2,1)S(1)}, bf16[128,256]{1,0:T(8,128)(2,1)S(1)}, u32[]{:S(2)}, u32[]{:S(2)}) collective-permute-start(bf16[128,256]{1,0:T(8,128)(2,1)S(1)} %get-tuple-element.60), channel_id=1, source_target_pairs={{0,6},{1,7},{2,4},{3,5},{4,2},{5,3},{6,0},{7,1},{8,14},{9,15},{10,... | collective-permute-start | bytes 196616 | tf_op jit(solution)/shard_map/ppermute | solution.py:277
